TPU v7x, 32 devices: a whole 2x2x4 slice. The times are simulated.
32 devices in a mesh: dom: 2 (over x), tok: 16 (over z, y, core).
Axes of the slice: x: 2, y: 2, z: 4, core: 2. Of those that a mesh axis runs over, the one named last changes fastest.
Arguments:
- tokens: bfloat16 [512, 4096], P(('dom', 'tok')), parts along dimension 0, may hold values from -6 to 6
- rotation_flip: int32 [4096], replicated, may hold values from 0 to 1
- gate_up: bfloat16 [4, 4096, 16384], P('dom', None, 'tok'), parts along dimension 0, may hold values from -0.09375 to 0.09375
- quant_codes: bfloat16 [4, 4096, 16384], P('dom', None, 'tok'), parts along dimension 0, may hold values from -7 to 7
- quant_exps: int32 [4, 32, 16384], P('dom', None, 'tok'), parts along dimension 0, may hold values from -10 to -7
- down_rows: bfloat16 [32768, 4096], P(('dom', 'tok')), parts along dimension 0, may hold values from -0.046875 to 0.046875
Outputs:
- correction: bfloat16 [32768, 4096], P(('dom', 'tok')), parts along dimension 0
There are 2 independent parts, one for each index of `dom`. A program takes and returns all parts, laid end to end along the dimension named above; an argument that names none is the same for every part. Nothing has to cross between parts.
All inputs are finite; a program needn't handle non-finite values.
Results may differ from a plain program's by a relative error of at most 0.012.
Values may be sent and summed in bfloat16 or wider, within the bound.
No kernel may reach another device: no remote copies, remote signals or barrier semaphores. Data moves between devices by JAX's collectives and lax.ppermute only.
A program may use at most 128 MiB of HBM per device.

v0:
```python
import jax
import jax.numpy as jnp
from jax import lax
from jax.sharding import PartitionSpec as P


def hadamard_table(order):
    index = jnp.arange(order, dtype=jnp.int32)
    common = index[:, None] & index[None, :]
    parity = jnp.zeros((order, order), jnp.int32)
    for bit_pos in range(max(order.bit_length() - 1, 1)):
        parity = parity ^ common >> bit_pos & 1
    return (1 - 2 * parity).astype(jnp.float32)


def rotate(inputs, flip):
    width = inputs.shape[-1]
    signed = inputs.astype(jnp.float32) * (1 - 2 * flip).astype(jnp.float32)
    power = width.bit_length() - 1
    outer_len = 2 ** (power // 2)
    inner_len = width // outer_len
    blocks = signed.reshape(-1, outer_len, inner_len)
    mixed = jnp.einsum(
        "ab,nbc,cd->nad",
        hadamard_table(outer_len),
        blocks,
        hadamard_table(inner_len),
        precision=lax.Precision.HIGHEST,
    )
    return (mixed.reshape(-1, width) * (1.0 / width**0.5)).astype(jnp.bfloat16)


def dequant(codes, exps):
    groups = exps.shape[1]
    scales = jnp.exp2(exps.astype(jnp.float32))
    shaped = codes.astype(jnp.float32).reshape(2, groups, codes.shape[1] // groups, codes.shape[2])
    return (shaped * scales[:, :, None, :]).reshape(codes.shape).astype(jnp.bfloat16)


def swiglu(inputs, weights):
    gate = jnp.dot(inputs, weights[0], preferred_element_type=jnp.float32)
    upper = jnp.dot(inputs, weights[1], preferred_element_type=jnp.float32)
    return (jax.nn.silu(gate) * upper).astype(jnp.bfloat16)


def per_device(tokens, rotation_flip, gate_up, quant_codes, quant_exps, down_rows):
    quant_weight = dequant(quant_codes, quant_exps)
    piece = lax.all_gather(tokens, "tok", axis=0, tiled=True)
    hid_full = swiglu(piece, gate_up)
    hid_quant = swiglu(rotate(piece, rotation_flip), quant_weight)
    mismatch = (hid_full.astype(jnp.float32) - hid_quant.astype(jnp.float32)).astype(jnp.bfloat16)
    total_tokens = mismatch.shape[0]
    partial_proj = jnp.dot(mismatch, down_rows, preferred_element_type=jnp.float32)
    projected = lax.psum(partial_proj, "tok").astype(jnp.bfloat16)
    gram = lax.dot_general(
        hid_quant, projected, (((0,), (0,)), ((), ())), preferred_element_type=jnp.float32
    )
    return (gram * (1.0 / total_tokens**0.5)).astype(jnp.bfloat16)


def solution(mesh):
    placed = (
        P(("dom", "tok"), None),
        P(),
        P("dom", None, "tok"),
        P("dom", None, "tok"),
        P("dom", None, "tok"),
        P(("dom", "tok"), None),
    )
    return jax.shard_map(
        per_device, mesh=mesh, in_specs=placed, out_specs=P(("dom", "tok"), None), check_vma=False
    )
```

profile of v0, /device:TPU:1, one launch (start us, length us, event | category | flops | bytes accessed | tf_op | source)
XLA Modules:
  0.0 203.8 jit_solution(15538142856855820026)
XLA Ops:
  6.5 0.0 all-gather.2.cloned.1.call-start
  6.5 0.7 all-gather.2.cloned.1.call-update
  7.3 1.0 multiply_exponential_fusion
  8.3 0.0 copy-start.2
  8.3 14.8 %fusion = bf16[2,4096,1024]{2,1,0:T(8,128)(2,1)} fusion(bf16[2,4096,1024]{2,1,0:T(8,128)(2,1)} %param.9, f32[2,32,1024]{2,1,0:T(8,128)S(1)} %multiply_exponential_fusion), kind=kLoop, calls=%fused_computation.1 | loop fusion | flops 25165824 | bytes 33816576 | tf_op jit(solution)/shard_map/convert_element_type | solution.py:37
  23.1 0.0 copy-done.2
  23.1 30.4 %all-gather.2.cloned.1.call-done = bf16[256,4096]{1,0:T(8,128)(2,1)} async-done(((bf16[16,4096]{1,0:T(8,128)(2,1)}), bf16[256,4096]{1,0:T(8,128)(2,1)}) %all-gather.2.cloned.1.call-update) | async-done | bytes 2097168 | tf_op jit(solution)/shard_map/all_gather | solution.py:48
  53.4 3.3 %copy.8 = bf16[256,4096]{0,1:T(8,128)(2,1)S(1)} copy(bf16[256,4096]{1,0:T(8,128)(2,1)} %all-gather.2.cloned.1.call-done) | data formatting | bytes 4194304 | tf_op jit(solution)/shard_map/all_gather | solution.py:48
  56.7 0.0 copy-start
  56.7 0.7 convert_multiply_fusion
  57.5 6.8 %fusion.11 = f32[256,64,64]{0,2,1:T(8,128)S(1)} fusion(f32[256,64,64]{0,2,1:T(8,128)S(1)} %bitcast.47), kind=kOutput, calls=%fused_computation.15 | convolution fusion | flops 805392384 | bytes 8388608 | tf_op jit(solution)/shard_map/ab,nbc,cd->nad/dot_general | solution.py:23
  64.2 6.0 %multiply_convert_fusion.1 = bf16[256,64,64]{0,2,1:T(8,128)(2,1)S(1)} fusion(f32[256,64,64]{0,2,1:T(8,128)S(1)} %fusion.11), kind=kOutput, calls=%fused_computation.17 | convolution fusion | flops 807489536 | bytes 6291456 | tf_op jit(solution)/shard_map/ab,nbc,cd->nad/dot_general | solution.py:23
  70.3 0.0 copy-done
  70.3 2.4 %fusion.2 = f32[256,1024]{1,0:T(8,128)S(1)} fusion(bf16[256,4096]{0,1:T(8,128)(2,1)S(1)} %bitcast.48, bf16[2,4096,1024]{2,1,0:T(8,128)(2,1)S(1)} %copy-done), kind=kOutput, calls=%fused_computation.6 | convolution fusion | flops 2147483648 | bytes 11534336 | tf_op jit(solution)/shard_map/dot_general | solution.py:41
  72.6 0.0 copy-start.1
  72.6 2.4 %fusion.20 = bf16[256,1024]{1,0:T(8,128)(2,1)S(1)} fusion(bf16[256,4096]{0,1:T(8,128)(2,1)S(1)} %bitcast.49, bf16[2,4096,1024]{2,1,0:T(8,128)(2,1)S(1)} %copy-done, f32[256,1024]{1,0:T(8,128)S(1)} %fusion.2), kind=kOutput, calls=%fused_computation.22 | convolution fusion | flops 2149056512 | bytes 12058624 | tf_op jit(solution)/shard_map/dot_general | solution.py:42
  75.1 0.0 copy-done.1
  75.1 6.7 %fusion.5 = f32[256,1024]{1,0:T(8,128)} fusion(bf16[256,4096]{1,0:T(8,128)(2,1)S(1)} %copy-done.1, bf16[2,4096,1024]{2,1,0:T(8,128)(2,1)} %param.8), kind=kOutput, calls=%fused_computation.9 | convolution fusion | flops 2147483648 | bytes 11534336 | tf_op jit(solution)/shard_map/dot_general | solution.py:41
  81.8 12.7 %fusion.34 = f32[256,4096]{1,0:T(8,128)} fusion(bf16[1024,4096]{1,0:T(8,128)(2,1)} %param.11, bf16[256,4096]{1,0:T(8,128)(2,1)S(1)} %copy-done.1, bf16[2,4096,1024]{2,1,0:T(8,128)(2,1)} %param.8, bf16[256,1024]{1,0:T(8,128)(2,1)S(1)} %fusion.20, f32[256,1024]{1,0:T(8,128)} %fusion.5), kind=kOutput, calls=%fused_computation.27 | convolution fusion | flops 4297588736 | bytes 24641536 | tf_op jit(solution)/shard_map/dot_general | solution.py:53
  94.5 96.6 %all-reduce.1 = bf16[256,4096]{1,0:T(8,128)(2,1)S(1)} all-reduce(f32[256,4096]{1,0:T(8,128)} %fusion.34), channel_id=1, replica_groups=mesh['dom'=2,'tok'=16] {'tok'}, use_global_device_ids=true, to_apply=%region_0.1 | all-reduce | flops 1048576 | bytes 6291456 | tf_op jit(solution)/shard_map/psum | solution.py:54
  191.1 5.8 %multiply_convert_fusion = bf16[1024,4096]{1,0:T(8,128)(2,1)} fusion(bf16[256,1024]{1,0:T(8,128)(2,1)S(1)} %fusion.20, bf16[256,4096]{1,0:T(8,128)(2,1)S(1)} %all-reduce.1), kind=kOutput, calls=%fused_computation.2 | convolution fusion | flops 2155872256 | bytes 11010048 | tf_op jit(solution)/shard_map/dot_general | solution.py:55
  (1 shorter events, 0.0 us)
Async XLA Ops:
  6.5 46.9 %all-gather.2.cloned.1.call-start = ((), (), s32[]{:S(2)}) async-start(), calls=%async_computation | async-start | bytes 2228224 | tf_op jit(solution)/shard_map/all_gather | solution.py:48
  8.3 14.8 %copy-start.2 = (s32[4096]{0:T(1024)S(1)}, s32[4096]{0:T(1024)}, u32[]{:S(2)}) copy-start(s32[4096]{0:T(1024)} %param.7) | copy-start | bytes 49156
  56.7 13.6 %copy-start = (bf16[2,4096,1024]{2,1,0:T(8,128)(2,1)S(1)}, bf16[2,4096,1024]{2,1,0:T(8,128)(2,1)}, u32[]{:S(2)}) copy-start(bf16[2,4096,1024]{2,1,0:T(8,128)(2,1)} %fusion) | copy-start | bytes 50331652
  72.6 2.5 %copy-start.1 = (bf16[256,4096]{1,0:T(8,128)(2,1)S(1)}, bf16[256,4096]{1,0:T(8,128)(2,1)}, u32[]{:S(2)}) copy-start(bf16[256,4096]{1,0:T(8,128)(2,1)} %all-gather.2.cloned.1.call-done) | copy-start | bytes 6291460
Sparse Core Ops, SparseCore 0:
  9.5 43.9 all-gather.1
where the time goes:
time: 204 us
  blocking collectives  96.6 us (47%)
  matrix products  42.8 us (21%)
  waiting for transfers between devices  31.1 us (15%)
  other arithmetic  16.5 us (8%)
  between operations  13.5 us (7%)
  local copies, waits for them, and re-layouts  3.28 us (2%)
    psum x1, blocking collectives, per_device(): projected = lax.psum(partial_proj, 'tok').astype(jnp.bfloat16)  96.6 us
    all_gather x1, waiting for transfers between devices, per_device(): piece = lax.all_gather(tokens, 'tok', axis=0, tiled=True)  30.4 us
    convert_element_type x1, other arithmetic, dequant(): (shaped * scales[:, :, None, :]).reshape(codes.shape).astype(jnp.bfloat16)  14.8 us
    dot_general x2, matrix products, rotate(): jnp.einsum('ab,nbc,cd->nad', hadamard_table(outer_len), blocks, hadamard_...  12.8 us
    dot_general x1, matrix products, per_device(): jnp.dot(mismatch, down_rows, preferred_element_type=jnp.float32)  12.7 us
    dot_general x2, matrix products, swiglu(): gate = jnp.dot(inputs, weights[0], preferred_element_type=jnp.float32)  9.03 us
    dot_general x1, matrix products, per_device(): lax.dot_general(hid_quant, projected, (((0,), (0,)), ((), ())), preferred...  5.79 us
  transfers between devices with their start and end apart: 1, of which 1 were waited for; matrix products, arithmetic and copies ran while one was open for 8% of the time, Pallas kernels for 0%

commit v1 on v0

--- a/solution.py
+++ b/solution.py
@@ -51,7 +51,7 @@
     mismatch = (hid_full.astype(jnp.float32) - hid_quant.astype(jnp.float32)).astype(jnp.bfloat16)
     total_tokens = mismatch.shape[0]
     partial_proj = jnp.dot(mismatch, down_rows, preferred_element_type=jnp.float32)
-    projected = lax.psum(partial_proj, "tok").astype(jnp.bfloat16)
+    projected = jnp.sum(lax.all_gather(partial_proj, "tok"), axis=0).astype(jnp.bfloat16)
     gram = lax.dot_general(
         hid_quant, projected, (((0,), (0,)), ((), ())), preferred_element_type=jnp.float32
     )

time: 204 us -> 454 us (2.23)
  waiting for transfers between devices: 31.1 us -> 356 us
  blocking collectives: 96.6 us -> 0 us
  other arithmetic: 16.5 us -> 37.8 us
    all_gather x0 -> x1, waiting for transfers between devices: none -> 325 us  [per_device(): lax.all_gather(partial_proj, 'tok')]
    psum x1 -> x0, blocking collectives: 96.6 us -> none  [per_device(): projected = lax.psum(partial_proj, 'tok').astype(jnp.bfloat16)]
    reduce_sum x0 -> x1, other arithmetic: none -> 21.3 us  [per_device(): jnp.sum(lax.all_gather(partial_proj, 'tok'), axis=0).astype(jnp.bfloat16)]
  transfers between devices with their start and end apart: 1 -> 2, of which waited for: 1 -> 2; matrix products, arithmetic and copies ran while one was open for 8% -> 3% of each run, Pallas kernels for 0% -> 0%
where the time goes in v1:
time: 454 us; the launch traced here: 453 us
  waiting for transfers between devices  356 us (78%)
  matrix products  42.8 us (9%)
  other arithmetic  37.8 us (8%)
  between operations  13.5 us (3%)
    all_gather x1, waiting for transfers between devices, per_device(): lax.all_gather(partial_proj, 'tok')  325 us
    all_gather x1, waiting for transfers between devices, per_device(): piece = lax.all_gather(tokens, 'tok', axis=0, tiled=True)  30.4 us
    reduce_sum x1, other arithmetic, per_device(): jnp.sum(lax.all_gather(partial_proj, 'tok'), axis=0).astype(jnp.bfloat16)  21.3 us
    convert_element_type x1, other arithmetic, dequant(): (shaped * scales[:, :, None, :]).reshape(codes.shape).astype(jnp.bfloat16)  14.8 us
    dot_general x2, matrix products, rotate(): jnp.einsum('ab,nbc,cd->nad', hadamard_table(outer_len), blocks, hadamard_...  12.8 us
    dot_general x1, matrix products, per_device(): jnp.dot(mismatch, down_rows, preferred_element_type=jnp.float32)  12.7 us
  transfers between devices with their start and end apart: 2, of which 2 were waited for; matrix products, arithmetic and copies ran while one was open for 3% of the time, Pallas kernels for 0%

profile of v1, /device:TPU:1, one launch (start us, length us, event | category | flops | bytes accessed | tf_op | source)
XLA Modules:
  0.0 453.5 jit_solution(15188079136583211345)
XLA Ops:
  6.5 0.0 all-gather.4.cloned.1.call-start
  6.5 0.7 all-gather.4.cloned.1.call-update
  7.3 0.0 all-gather.6.cloned.1.call-start
  7.3 1.0 multiply_exponential_fusion
  8.3 0.0 copy-start.2
  8.3 14.8 %fusion = bf16[2,4096,1024]{2,1,0:T(8,128)(2,1)} fusion(bf16[2,4096,1024]{2,1,0:T(8,128)(2,1)} %param.9, f32[2,32,1024]{2,1,0:T(8,128)S(1)} %multiply_exponential_fusion), kind=kLoop, calls=%fused_computation.1 | loop fusion | flops 25165824 | bytes 33816576 | tf_op jit(solution)/shard_map/convert_element_type | solution.py:37
  23.1 0.0 copy-done.2
  23.1 30.4 %all-gather.4.cloned.1.call-done = bf16[256,4096]{1,0:T(8,128)(2,1)} async-done(((bf16[16,4096]{1,0:T(8,128)(2,1)}), bf16[256,4096]{1,0:T(8,128)(2,1)}) %all-gather.4.cloned.1.call-update) | async-done | bytes 2097168 | tf_op jit(solution)/shard_map/all_gather | solution.py:48
  53.4 3.3 copy.8
  56.7 0.0 copy-start
  56.7 0.7 convert_multiply_fusion
  57.5 6.8 %fusion.11 = f32[256,64,64]{0,2,1:T(8,128)S(1)} fusion(f32[256,64,64]{0,2,1:T(8,128)S(1)} %bitcast.48), kind=kOutput, calls=%fused_computation.15 | convolution fusion | flops 805392384 | bytes 8388608 | tf_op jit(solution)/shard_map/ab,nbc,cd->nad/dot_general | solution.py:23
  64.2 6.0 %multiply_convert_fusion.1 = bf16[256,64,64]{0,2,1:T(8,128)(2,1)S(1)} fusion(f32[256,64,64]{0,2,1:T(8,128)S(1)} %fusion.11), kind=kOutput, calls=%fused_computation.17 | convolution fusion | flops 807489536 | bytes 6291456 | tf_op jit(solution)/shard_map/ab,nbc,cd->nad/dot_general | solution.py:23
  70.3 0.0 copy-done
  70.3 2.4 fusion.2
  72.6 0.0 copy-start.1
  72.6 2.4 fusion.20
  75.1 0.0 copy-done.1
  75.1 6.7 %fusion.5 = f32[256,1024]{1,0:T(8,128)} fusion(bf16[256,4096]{1,0:T(8,128)(2,1)S(1)} %copy-done.1, bf16[2,4096,1024]{2,1,0:T(8,128)(2,1)} %param.8), kind=kOutput, calls=%fused_computation.9 | convolution fusion | flops 2147483648 | bytes 11534336 | tf_op jit(solution)/shard_map/dot_general | solution.py:41
  81.8 12.7 %fusion.34 = f32[256,4096]{1,0:T(8,128)} fusion(bf16[1024,4096]{1,0:T(8,128)(2,1)} %param.11, bf16[256,4096]{1,0:T(8,128)(2,1)S(1)} %copy-done.1, bf16[2,4096,1024]{2,1,0:T(8,128)(2,1)} %param.8, bf16[256,1024]{1,0:T(8,128)(2,1)S(1)} %fusion.20, f32[256,1024]{1,0:T(8,128)} %fusion.5), kind=kOutput, calls=%fused_computation.27 | convolution fusion | flops 4297588736 | bytes 24641536 | tf_op jit(solution)/shard_map/dot_general | solution.py:53
  94.5 0.0 all-gather.6.cloned.1.call-update
  94.5 325.0 %all-gather.6.cloned.1.call-done = f32[4096,4096]{1,0:T(8,128)} async-done(((f32[256,4096]{1,0:T(8,128)}), f32[4096,4096]{1,0:T(8,128)}) %all-gather.6.cloned.1.call-update) | async-done | bytes 67108880 | tf_op jit(solution)/shard_map/all_gather | solution.py:54
  419.5 21.3 %reduce_sum.9 = bf16[256,4096]{1,0:T(8,128)(2,1)S(1)} reduce(f32[16,256,4096]{2,1,0:T(8,128)} %bitcast.9, f32[]{:T(128)} %constant.9.clone.1), dimensions={0}, to_apply=%region_0.1 | reduce | flops 15728640 | bytes 69206016 | tf_op jit(solution)/shard_map/reduce_sum | solution.py:54
  440.8 5.8 %multiply_convert_fusion = bf16[1024,4096]{1,0:T(8,128)(2,1)} fusion(bf16[256,1024]{1,0:T(8,128)(2,1)S(1)} %fusion.20, bf16[256,4096]{1,0:T(8,128)(2,1)S(1)} %reduce_sum.9), kind=kOutput, calls=%fused_computation.2 | convolution fusion | flops 2155872256 | bytes 11010048 | tf_op jit(solution)/shard_map/dot_general | solution.py:55
  (1 shorter events, 0.0 us)
Async XLA Ops:
  6.5 46.9 %all-gather.4.cloned.1.call-start = ((), (), s32[]{:S(2)}) async-start(), calls=%async_computation | async-start | bytes 2228224 | tf_op jit(solution)/shard_map/all_gather | solution.py:48
  7.3 412.2 %all-gather.6.cloned.1.call-start = ((), (), s32[]{:S(2)}) async-start(), calls=%async_computation.1 | async-start | bytes 71303168 | tf_op jit(solution)/shard_map/all_gather | solution.py:54
  8.3 14.8 %copy-start.2 = (s32[4096]{0:T(1024)S(1)}, s32[4096]{0:T(1024)}, u32[]{:S(2)}) copy-start(s32[4096]{0:T(1024)} %param.7) | copy-start | bytes 49156
  56.7 13.6 %copy-start = (bf16[2,4096,1024]{2,1,0:T(8,128)(2,1)S(1)}, bf16[2,4096,1024]{2,1,0:T(8,128)(2,1)}, u32[]{:S(2)}) copy-start(bf16[2,4096,1024]{2,1,0:T(8,128)(2,1)} %fusion) | copy-start | bytes 50331652
  72.6 2.5 copy-start.1
Sparse Core Ops, SparseCore 0:
  9.5 43.9 all-gather.3
  94.6 324.7 all-gather.5
